TPU v7x, 32 devices: a whole 2x2x4 slice. The times are simulated.
32 devices in a mesh: grp: 2 (over y), kz: 4 (over z), coil: 2 (over x), kx: 2 (over core).
Axes of the slice: x: 2, y: 2, z: 4, core: 2. Of those that a mesh axis runs over, the one named last changes fastest.
Arguments:
- measured: float32 [2, 64, 32, 32, 32], P(None, ('grp', 'coil'), 'kx', 'kz'), parts along dimension 1, may hold values from -6 to 6
- mask: int32 [64, 32, 32], P(('grp', 'kx'), 'kz'), parts along dimension 0, may hold values 0 or 1
- kernel: float32 [27, 2, 32, 64], P(None, None, 'coil'), may hold values from -0.109375 to 0.109375
Outputs:
- restored: float32 [2, 64, 32, 32, 32], P(None, ('grp', 'coil'), 'kx', 'kz'), parts along dimension 1
There are 2 independent parts, one for each index of `grp`. A program takes and returns all parts, laid end to end along the dimension named above; an argument that names none is the same for every part. Nothing has to cross between parts.
All inputs are finite; a program needn't handle non-finite values. No bound on the sum of `mask` on one device may be relied on, other than what follows from the above.
Results may differ from a plain program's by a relative error of at most 0.0001.
Values sent between devices are 32-bit elements; how exact they have to be, the bound alone decides.
A program may use at most 128 MiB of HBM per device.

v0:
```python
import jax
import jax.numpy as jnp
from jax import lax
from jax.sharding import PartitionSpec as P

ITERS = 2


def partner(array, axis, apart):
    return lax.ppermute(array, axis, [(i, i ^ 1 << apart) for i in range(lax.axis_size(axis))])


def padded_2(array, sides, width):
    for axis, dim in sides:
        peers, length = (lax.axis_size(axis), array.shape[dim])
        up = [(i, (i + 1) % peers) for i in range(peers - 1)]
        down = [(j, i) for i, j in up]
        last = lax.slice_in_dim(array, length - width, length, axis=dim)
        first = lax.slice_in_dim(array, 0, width, axis=dim)
        before = lax.ppermute(last, axis, up)
        after = lax.ppermute(first, axis, down)
        array = jnp.concatenate([before, array, after], axis=dim)
    return array


def build_weights(kernel_part):
    real_k = kernel_part[:, 0]
    imag_k = kernel_part[:, 1]
    return jnp.concatenate(
        [jnp.concatenate([real_k, -imag_k], 2), jnp.concatenate([imag_k, real_k], 2)], 1
    )


def convolve(padded, weights, rows, depth, width):
    padded = jnp.pad(padded, ((0, 0), (0, 0), (0, 0), (0, 0), (1, 1)))
    shape = padded.shape
    line = width + 2
    plane = (depth + 2) * line
    extra = 2 * line + 2
    flat = padded.reshape(shape[0] * shape[1], -1)
    flat = jnp.pad(flat, ((0, 0), (0, extra)))
    out_rows = weights.shape[1]
    length = rows * plane
    result = jnp.zeros((out_rows, length), jnp.float32)
    for first in range(3):
        window = flat[:, first * plane : first * plane + length + extra]
        group = weights[9 * first : 9 * first + 9].reshape(9 * out_rows, -1)
        products = jnp.dot(group, window, precision=lax.Precision.HIGHEST)
        products = products.reshape(9, out_rows, length + extra)
        for second in range(3):
            for third in range(3):
                offset = third * line + second
                result = result + products[3 * second + third, :, offset : offset + length]
    result = result.reshape(2, out_rows // 2, rows, depth + 2, line)
    return result[:, :, :, :depth, :width]


def on_device(measured, mask, kernel):
    sampled = (mask == 1)[None, None]
    state = jnp.where(sampled, measured, jnp.zeros_like(measured))
    weights = build_weights(kernel)
    sign = jnp.array([1.0, -1.0], jnp.float32).reshape(2, 1, 1, 1, 1)
    kz_bits = lax.axis_size("kz").bit_length() - 1
    rows = measured.shape[2]
    depth = measured.shape[3]
    width = measured.shape[4]
    for step in range(ITERS):
        mirrored = state
        for bit in range(kz_bits):
            mirrored = partner(mirrored, "kz", bit)
        bit = 0
        mirrored = partner(mirrored, "kx", bit)
        own_virtual = jnp.flip(mirrored, (2, 3, 4)) * sign
        physical, virtual = (
            lax.all_gather(state, "coil", axis=1, tiled=True),
            lax.all_gather(own_virtual, "coil", axis=1, tiled=True),
        )
        stacked = jnp.concatenate([physical, virtual], 1)
        padded = padded_2(stacked, (("kz", 3), ("kx", 2)), 1)
        result = convolve(padded, weights, rows, depth, width)
        state = jnp.where(sampled, measured, result)
    return state


def solution(mesh):
    placed = (
        P(None, ("grp", "coil"), "kx", "kz", None),
        P(("grp", "kx"), "kz", None),
        P(None, None, "coil", None),
    )
    return jax.shard_map(
        on_device,
        mesh=mesh,
        in_specs=placed,
        out_specs=P(None, ("grp", "coil"), "kx", "kz", None),
        check_vma=False,
    )
```

profile of v0, /device:TPU:9, one launch (start us, length us, event | category | flops | bytes accessed | tf_op | source)
XLA Modules:
  0.0 726.6 jit_solution(10788578500702772405)
XLA Ops:
  9.2 46.6 %collective-permute-done = f32[2,16,16,8,32]{4,3,2,1,0:T(8,128)} collective-permute-done((f32[2,16,16,8,32]{4,3,2,1,0:T(8,128)S(1)}, f32[2,16,16,8,32]{4,3,2,1,0:T(8,128)}, u32[]{:S(2)}, u32[]{:S(2)}) %collective-permute-start) | collective-permute-done | bytes 524320 | tf_op jit(solution)/shard_map/ppermute | solution.py:10
  58.2 90.4 %collective-permute-done.1 = f32[2,16,16,8,32]{4,3,2,1,0:T(8,128)} collective-permute-done((f32[2,16,16,8,32]{4,3,2,1,0:T(8,128)}, f32[2,16,16,8,32]{4,3,2,1,0:T(8,128)}, u32[]{:S(2)}, u32[]{:S(2)}) %collective-permute-start.1) | collective-permute-done | bytes 524320 | tf_op jit(solution)/shard_map/ppermute | solution.py:10
  162.5 53.6 %all-gather.7.cloned.1.call-done = f32[2,32,16,8,32]{4,3,2,1,0:T(8,128)} async-done(((f32[2,16,16,8,32]{4,3,2,1,0:T(8,128)}), f32[2,32,16,8,32]{4,3,2,1,0:T(8,128)}) %all-gather.7.cloned.1.call-update) | async-done | bytes 1048592 | tf_op jit(solution)/shard_map/all_gather | solution.py:76
  220.8 8.2 %fusion.16 = (f32[2,64,16,1,32]{4,3,2,1,0:T(1,128)S(1)}, f32[2,64,16,1,32]{4,3,2,1,0:T(1,128)S(1)}) fusion(f32[2,64,16,8,32]{4,3,2,1,0:T(8,128)} %constant_dynamic-update-slice_fusion), kind=kLoop, calls=%fused_computation.85 | loop fusion | bytes 1048576 | tf_op jit(solution)/shard_map/slice | solution.py:18
  235.6 7.8 %copy.17 = f32[2,64,16,8,32]{1,4,3,2,0:T(8,128)} copy(f32[2,64,16,8,32]{4,3,2,1,0:T(8,128)} %constant_dynamic-update-slice_fusion) | data formatting | bytes 4194304 | tf_op jit(solution)/shard_map/concatenate | solution.py:78
  255.8 8.4 %copy.25 = f32[2,64,18,10,32]{1,0,4,3,2:T(2,128)} copy(f32[2,64,18,10,32]{1,4,3,2,0:T(8,128)S(1)} %pad_maximum_fusion) | data formatting | bytes 5898240
  264.2 7.4 %pad.14.clone = f32[2,64,18,10,34]{1,0,4,3,2:T(2,128)} pad(f32[2,64,18,10,32]{1,0,4,3,2:T(2,128)} %copy.25, f32[]{:T(128)} %constant.2.clone.1), padding=0_0x0_0x0_0x0_0x1_1 | pad | bytes 6082564 | tf_op jit(solution)/shard_map/jit(_pad)/pad | solution.py:35
  271.7 6.2 reshape.97
  277.9 6.2 fusion.8
  289.3 7.3 %fusion.1 = f32[9,32,5510]{2,1,0:T(8,128)} fusion(f32[27,32,128]{2,1,0:T(8,128)S(1)} %copy-done.7, f32[128,6120]{0,1:T(8,128)S(1)} %reshape.97), kind=kOutput, calls=%fused_computation.7 | convolution fusion | flops 2437447680 | bytes 9923328 | tf_op jit(solution)/shard_map/dot_general | solution.py:48
  346.1 11.6 %add_add_fusion.1 = f32[2,16,16,10,34]{4,3,2,1,0:T(8,128)} fusion(f32[2,16,16,10,34]{4,3,2,1,0:T(8,128)} %squeeze.165, f32[2,16,16,10,34]{4,3,2,1,0:T(8,128)} %squeeze.164, f32[2,16,16,10,34]{4,3,2,1,0:T(8,128)} %squeeze.163, f32[2,16,16,10,34]{4,3,2,1,0:T(8,128)} %reshape.121, f32[2,16,16,10,34]{4,3,2,1,0:T(8,128)} %squeeze.162), kind=kLoop, calls=%fused_computation.3 | loop fusion | flops 696320 | bytes 4177920 | tf_op jit(solution)/shard_map/add | solution.py:53
  357.7 7.8 %fusion.11 = f32[2,16,16,8,32]{4,3,2,1,0:T(8,128)} fusion(f32[2,16,16,8,32]{4,3,2,1,0:T(8,128)S(1)} %copy-done.2, f32[2,16,16,10,34]{4,3,2,1,0:T(8,128)} %squeeze.171, f32[2,16,16,10,34]{4,3,2,1,0:T(8,128)} %squeeze.170, f32[2,16,16,10,34]{4,3,2,1,0:T(8,128)} %squeeze.169, f32[2,16,16,10,34]{4,3,2,1,0:T(8,128)} %squeeze.168, ...), kind=kLoop, calls=%fused_computation.26 | loop fusion | flops 917504 | bytes 4722688 | tf_op jit(solution)/shard_map/jit(_where)/select_n | solution.py:81
  365.7 46.8 %collective-permute-done.7 = f32[2,16,16,8,32]{4,3,2,1,0:T(8,128)} collective-permute-done((f32[2,16,16,8,32]{4,3,2,1,0:T(8,128)}, f32[2,16,16,8,32]{4,3,2,1,0:T(8,128)}, u32[]{:S(2)}, u32[]{:S(2)}) %collective-permute-start.7) | collective-permute-done | bytes 524320 | tf_op jit(solution)/shard_map/ppermute | solution.py:10
  413.8 89.6 %collective-permute-done.8 = f32[2,16,16,8,32]{4,3,2,1,0:T(8,128)S(1)} collective-permute-done((f32[2,16,16,8,32]{4,3,2,1,0:T(8,128)}, f32[2,16,16,8,32]{4,3,2,1,0:T(8,128)S(1)}, u32[]{:S(2)}, u32[]{:S(2)}) %collective-permute-start.8) | collective-permute-done | bytes 524320 | tf_op jit(solution)/shard_map/ppermute | solution.py:10
  518.1 52.6 %all-gather.11.cloned.1.call-done = f32[2,32,16,8,32]{4,3,2,1,0:T(8,128)} async-done(((f32[2,16,16,8,32]{4,3,2,1,0:T(8,128)}), f32[2,32,16,8,32]{4,3,2,1,0:T(8,128)}) %all-gather.11.cloned.1.call-update) | async-done | bytes 1048592 | tf_op jit(solution)/shard_map/all_gather | solution.py:76
  575.4 8.3 %fusion.15 = (f32[2,64,16,1,32]{4,3,2,1,0:T(1,128)S(1)}, f32[2,64,16,1,32]{4,3,2,1,0:T(1,128)S(1)}) fusion(f32[2,64,16,8,32]{4,3,2,1,0:T(8,128)} %constant_dynamic-update-slice_fusion.2), kind=kLoop, calls=%fused_computation.84 | loop fusion | bytes 1048576 | tf_op jit(solution)/shard_map/slice | solution.py:18
  590.3 7.9 %copy.21 = f32[2,64,16,8,32]{1,4,3,2,0:T(8,128)} copy(f32[2,64,16,8,32]{4,3,2,1,0:T(8,128)} %constant_dynamic-update-slice_fusion.2) | data formatting | bytes 4194304 | tf_op jit(solution)/shard_map/concatenate | solution.py:78
  610.6 8.4 %copy.26 = f32[2,64,18,10,32]{1,0,4,3,2:T(2,128)} copy(f32[2,64,18,10,32]{1,4,3,2,0:T(8,128)S(1)} %pad_maximum_fusion.1) | data formatting | bytes 5898240
  619.0 7.4 %pad.16.clone = f32[2,64,18,10,34]{1,0,4,3,2:T(2,128)} pad(f32[2,64,18,10,32]{1,0,4,3,2:T(2,128)} %copy.26, f32[]{:T(128)} %constant.2.clone.1), padding=0_0x0_0x0_0x0_0x1_1 | pad | bytes 6082564 | tf_op jit(solution)/shard_map/jit(_pad)/pad | solution.py:35
  626.4 6.2 reshape.98
  632.6 6.2 fusion.6
  644.1 7.3 %fusion.4 = f32[9,32,5510]{2,1,0:T(8,128)} fusion(f32[27,32,128]{2,1,0:T(8,128)S(1)} %copy-done.8, f32[128,6120]{0,1:T(8,128)S(1)} %reshape.98), kind=kOutput, calls=%fused_computation.9 | convolution fusion | flops 2437447680 | bytes 9923328 | tf_op jit(solution)/shard_map/dot_general | solution.py:48
  700.5 11.6 %add_add_fusion = f32[2,16,16,10,34]{4,3,2,1,0:T(8,128)} fusion(f32[2,16,16,10,34]{4,3,2,1,0:T(8,128)} %squeeze.187, f32[2,16,16,10,34]{4,3,2,1,0:T(8,128)} %squeeze.186, f32[2,16,16,10,34]{4,3,2,1,0:T(8,128)} %squeeze.185, f32[2,16,16,10,34]{4,3,2,1,0:T(8,128)} %reshape.122, f32[2,16,16,10,34]{4,3,2,1,0:T(8,128)} %squeeze.184), kind=kLoop, calls=%fused_computation.2 | loop fusion | flops 696320 | bytes 4177920 | tf_op jit(solution)/shard_map/add | solution.py:53
  712.1 7.8 %fusion.10 = f32[2,16,16,8,32]{4,3,2,1,0:T(8,128)} fusion(f32[2,16,16,8,32]{4,3,2,1,0:T(8,128)S(1)} %copy-done.3, f32[2,16,16,10,34]{4,3,2,1,0:T(8,128)} %squeeze.193, f32[2,16,16,10,34]{4,3,2,1,0:T(8,128)} %squeeze.192, f32[2,16,16,10,34]{4,3,2,1,0:T(8,128)} %squeeze.191, f32[2,16,16,10,34]{4,3,2,1,0:T(8,128)} %squeeze.190, ...), kind=kLoop, calls=%fused_computation.19 | loop fusion | flops 917504 | bytes 4722688 | tf_op jit(solution)/shard_map/jit(_where)/select_n | solution.py:81
  (105 shorter events, 191.3 us)
Async XLA Ops:
  6.5 151.3 %all-gather.5.cloned.1.call-start = ((), (), s32[]{:S(2)}) async-start(), calls=%async_computation | async-start | bytes 6291456 | tf_op jit(solution)/shard_map/all_gather | solution.py:75
  9.1 49.0 %copy-start.6 = (f32[2,16,16,8,32]{4,3,2,1,0:T(8,128)}, f32[2,16,16,8,32]{4,3,2,1,0:T(8,128)S(1)}, u32[]{:S(2)}) copy-start(f32[2,16,16,8,32]{4,3,2,1,0:T(8,128)S(1)} %broadcast_select_fusion) | copy-start | bytes 1572868
  9.2 146.9 %copy-start.10 = (f32[2]{0:T(128)S(1)}, f32[2]{0:T(128)}, u32[]{:S(2)}) copy-start(f32[2]{0:T(128)} %constant.8.clone) | copy-start | bytes 28
  9.2 46.7 %collective-permute-start = (f32[2,16,16,8,32]{4,3,2,1,0:T(8,128)S(1)}, f32[2,16,16,8,32]{4,3,2,1,0:T(8,128)}, u32[]{:S(2)}, u32[]{:S(2)}) collective-permute-start(f32[2,16,16,8,32]{4,3,2,1,0:T(8,128)S(1)} %broadcast_select_fusion), channel_id=1, source_target_pairs={{0,4},{4,0},{8,12},{12,8},{1,5},{5,1},{9,13},{13,9},{2,6},{6,2},{1... | collective-permute-start | bytes 1572872 | tf_op jit(solution)/shard_map/ppermute | solution.py:10
  55.9 92.8 %collective-permute-start.1 = (f32[2,16,16,8,32]{4,3,2,1,0:T(8,128)}, f32[2,16,16,8,32]{4,3,2,1,0:T(8,128)}, u32[]{:S(2)}, u32[]{:S(2)}) collective-permute-start(f32[2,16,16,8,32]{4,3,2,1,0:T(8,128)} %collective-permute-done), channel_id=1, source_target_pairs={{0,8},{4,12},{8,0},{12,4},{1,9},{5,13},{9,1},{13,5},{2,10},{6,14},... | collective-permute-start | bytes 1572872 | tf_op jit(solution)/shard_map/ppermute | solution.py:10
  58.2 157.9 %all-gather.7.cloned.1.call-start = ((), (), s32[]{:S(2)}) async-start(), calls=%async_computation.1 | async-start | bytes 6291456 | tf_op jit(solution)/shard_map/all_gather | solution.py:76
  148.7 4.6 collective-permute-start.2
  157.7 355.6 %all-gather.9.cloned.1.call-start = ((), (), s32[]{:S(2)}) async-start(), calls=%async_computation.2 | async-start | bytes 6291456 | tf_op jit(solution)/shard_map/all_gather | solution.py:75
  220.8 14.7 %copy-start.9 = (f32[27,2,16,64]{3,2,1,0:T(8,128)S(1)}, f32[27,2,16,64]{3,2,1,0:T(8,128)}, u32[]{:S(2)}) copy-start(f32[27,2,16,64]{3,2,1,0:T(8,128)} %param.6) | copy-start | bytes 663556
  229.6 14.5 %collective-permute-start.3 = (f32[2,64,16,1,32]{1,4,3,2,0:T(8,128)S(1)}, f32[2,64,16,1,32]{1,4,3,2,0:T(8,128)S(1)}, u32[]{:S(2)}, u32[]{:S(2)}) collective-permute-start(f32[2,64,16,1,32]{1,4,3,2,0:T(8,128)S(1)} %copy.15), channel_id=1, source_target_pairs={{0,4},{4,8},{8,12},{1,5},{5,9},{9,13},{2,6},{6,10},{10,14},{3,7},{... | collective-permute-start | bytes 786440 | tf_op jit(solution)/shard_map/ppermute | solution.py:20
  233.3 14.3 %collective-permute-start.4 = (f32[2,64,16,1,32]{1,4,3,2,0:T(8,128)S(1)}, f32[2,64,16,1,32]{1,4,3,2,0:T(8,128)S(1)}, u32[]{:S(2)}, u32[]{:S(2)}) collective-permute-start(f32[2,64,16,1,32]{1,4,3,2,0:T(8,128)S(1)} %copy.16), channel_id=1, source_target_pairs={{4,0},{8,4},{12,8},{5,1},{9,5},{13,9},{6,2},{10,6},{14,10},{7,3},{... | collective-permute-start | bytes 786440 | tf_op jit(solution)/shard_map/ppermute | solution.py:21
  243.4 11.8 %copy-start = (f32[2,64,16,8,32]{1,4,3,2,0:T(8,128)S(1)}, f32[2,64,16,8,32]{1,4,3,2,0:T(8,128)}, u32[]{:S(2)}) copy-start(f32[2,64,16,8,32]{1,4,3,2,0:T(8,128)} %copy.17) | copy-start | bytes 6291460
  248.7 6.4 collective-permute-start.5
  250.0 5.1 collective-permute-start.6
  346.1 11.6 %copy-start.5 = (f32[2,16,16,10,34]{4,3,2,1,0:T(8,128)S(1)}, f32[2,16,16,10,34]{4,3,2,1,0:T(8,128)}, u32[]{:S(2)}) copy-start(f32[2,16,16,10,34]{4,3,2,1,0:T(8,128)} %squeeze.166) | copy-start | bytes 2088964
  365.4 47.1 %collective-permute-start.7 = (f32[2,16,16,8,32]{4,3,2,1,0:T(8,128)}, f32[2,16,16,8,32]{4,3,2,1,0:T(8,128)}, u32[]{:S(2)}, u32[]{:S(2)}) collective-permute-start(f32[2,16,16,8,32]{4,3,2,1,0:T(8,128)} %fusion.11), channel_id=1, source_target_pairs={{0,4},{4,0},{8,12},{12,8},{1,5},{5,1},{9,13},{13,9},{2,6},{6,2},{1... | collective-permute-start | bytes 1572872 | tf_op jit(solution)/shard_map/ppermute | solution.py:10
  412.6 90.9 %collective-permute-start.8 = (f32[2,16,16,8,32]{4,3,2,1,0:T(8,128)}, f32[2,16,16,8,32]{4,3,2,1,0:T(8,128)S(1)}, u32[]{:S(2)}, u32[]{:S(2)}) collective-permute-start(f32[2,16,16,8,32]{4,3,2,1,0:T(8,128)} %collective-permute-done.7), channel_id=1, source_target_pairs={{0,8},{4,12},{8,0},{12,4},{1,9},{5,13},{9,1},{13,5},{2,10},{6,14},... | collective-permute-start | bytes 1572872 | tf_op jit(solution)/shard_map/ppermute | solution.py:10
  413.8 156.9 %all-gather.11.cloned.1.call-start = ((), (), s32[]{:S(2)}) async-start(), calls=%async_computation.3 | async-start | bytes 6291456 | tf_op jit(solution)/shard_map/all_gather | solution.py:76
  503.5 5.3 collective-permute-start.9
  584.3 14.5 %collective-permute-start.10 = (f32[2,64,16,1,32]{1,4,3,2,0:T(8,128)S(1)}, f32[2,64,16,1,32]{1,4,3,2,0:T(8,128)S(1)}, u32[]{:S(2)}, u32[]{:S(2)}) collective-permute-start(f32[2,64,16,1,32]{1,4,3,2,0:T(8,128)S(1)} %copy.19), channel_id=1, source_target_pairs={{0,4},{4,8},{8,12},{1,5},{5,9},{9,13},{2,6},{6,10},{10,14},{3,7},{... | collective-permute-start | bytes 786440 | tf_op jit(solution)/shard_map/ppermute | solution.py:20
  588.1 14.3 %collective-permute-start.11 = (f32[2,64,16,1,32]{1,4,3,2,0:T(8,128)S(1)}, f32[2,64,16,1,32]{1,4,3,2,0:T(8,128)S(1)}, u32[]{:S(2)}, u32[]{:S(2)}) collective-permute-start(f32[2,64,16,1,32]{1,4,3,2,0:T(8,128)S(1)} %copy.20), channel_id=1, source_target_pairs={{4,0},{8,4},{12,8},{5,1},{9,5},{13,9},{6,2},{10,6},{14,10},{7,3},{... | collective-permute-start | bytes 786440 | tf_op jit(solution)/shard_map/ppermute | solution.py:21
  598.1 11.7 %copy-start.1 = (f32[2,64,16,8,32]{1,4,3,2,0:T(8,128)S(1)}, f32[2,64,16,8,32]{1,4,3,2,0:T(8,128)}, u32[]{:S(2)}) copy-start(f32[2,64,16,8,32]{1,4,3,2,0:T(8,128)} %copy.21) | copy-start | bytes 6291460
  603.4 5.2 collective-permute-start.12
  604.7 5.1 collective-permute-start.13
  (5 other events, 47.3 us)
Sparse Core Ops, SparseCore 0:
  58.3 56.8 all-gather.4
  157.9 58.1 all-gather.6
  413.9 56.4 all-gather.8
  513.5 57.1 all-gather.10
where the time goes:
time: 734 us; the launch traced here: 727 us
  waiting for transfers between devices  397 us (54%)
  local copies, waits for them, and re-layouts  196 us (27%)
  other arithmetic  55.1 us (8%)
  matrix products  37.4 us (5%)
  starting transfers between devices  27.1 us (4%)
  between operations  13.7 us (2%)
    ppermute x6, waiting for transfers between devices, partner(): lax.ppermute(array, axis, [(i, i ^ 1 << apart) for i in range(lax.axis_si...  282 us
    all_gather x2, waiting for transfers between devices, on_device(): lax.all_gather(own_virtual, 'coil', axis=1, tiled=True)  106 us
    squeeze x20, local copies, waits for them, and re-layouts, convolve(): result = result + products[3 * second + third, :, offset:offset + length]  74.1 us
    dot_general x6, matrix products, convolve(): products = jnp.dot(group, window, precision=lax.Precision.HIGHEST)  37.4 us
    unnamed x26, local copies, waits for them, and re-layouts  26.3 us
    concatenate x4, local copies, waits for them, and re-layouts, on_device(): stacked = jnp.concatenate([physical, virtual], 1)  25.1 us
    add x2, other arithmetic, convolve(): result = result + products[3 * second + third, :, offset:offset + length]  23.2 us
    slice x4, local copies, waits for them, and re-layouts, padded_2(): last = lax.slice_in_dim(array, length - width, length, axis=dim)  17.7 us
  transfers between devices with their start and end apart: 18, of which 13 were waited for; matrix products, arithmetic and copies ran while one was open for 5% of the time, Pallas kernels for 0%

commit v1 on v0

v1 whole, which is shorter than its diff:
```python
import functools

import jax
import jax.numpy as jnp
from jax import lax
from jax.experimental import pallas as pl
from jax.experimental.pallas import tpu as pltpu
from jax.sharding import PartitionSpec as P

ITERS = 2
LANES = 128
MESH = pl.DeviceIdType.MESH


def build_weights(kernel, shards):
    coils = kernel.shape[2]
    k = kernel.reshape(3, 3, 3, 2, coils, 2, shards, coils)
    re, im = k[:, :, :, 0], k[:, :, :, 1]
    pr, pi = re[:, :, :, :, 0], im[:, :, :, :, 0]
    vr, vi = (jnp.flip(x[:, :, :, :, 1], (0, 1, 2)) for x in (re, im))

    def block(q):
        return jnp.stack([jnp.stack(row, 0) for row in q], 0)

    w = jnp.stack([block(((pr, -pi), (pi, pr))), block(((vr, vi), (vi, -vr)))], 0)
    w = w.transpose(0, 4, 3, 1, 6, 5, 7, 2, 8)
    return w.reshape(36 * coils, 6 * shards * coils)


def split(x):
    hi = x.astype(jnp.bfloat16)
    return hi, (x - hi.astype(jnp.float32)).astype(jnp.bfloat16)


def body(sizes, row, measured, mask, weights, out, x, xh, xl, wh, wl, r1, r2, rm,
         g_send, g_recv, z_send, z_recv, k_send, k_recv, m_send, m_recv):
    nz, nc = sizes
    planes, rows, lanes = measured.shape
    wide = lanes + LANES
    z, c, h = lax.axis_index("kz"), lax.axis_index("coil"), lax.axis_index("kx")
    mirror = {"kz": nz - 1 - z, "kx": 1 - h}

    barrier = pltpu.get_barrier_semaphore()
    for d in range(1, nc):
        pl.semaphore_signal(barrier, inc=1, device_id={"coil": lax.rem(c + d, nc)}, device_id_type=MESH)
    pl.semaphore_signal(barrier, inc=1, device_id={"kx": 1 - h}, device_id_type=MESH)
    pl.semaphore_signal(barrier, inc=1, device_id=mirror, device_id_type=MESH)

    for d in (1, nz - 1):
        pl.semaphore_signal(barrier, inc=1, device_id={"kz": lax.rem(z + d, nz)}, device_id_type=MESH)
    pl.semaphore_wait(barrier, nc + 3)

    lane = lax.broadcasted_iota(jnp.int32, (1, wide), 1)
    edge = lane - lanes - h * (LANES - row)
    keep = (lane < lanes) | ((edge >= 0) & (edge < row))
    column = lax.rem(lane, row)
    after, before = column > 0, column < row - 1
    flip = (lax.broadcasted_iota(jnp.int32, (LANES, LANES), 0)
            + lax.broadcasted_iota(jnp.int32, (LANES, LANES), 1) == LANES - 1)
    flip = flip.astype(jnp.float32).astype(jnp.bfloat16)

    def remote(src, dst, send, recv, device):
        return pltpu.make_async_remote_copy(
            src_ref=src, dst_ref=dst, send_sem=send, recv_sem=recv, device_id=device, device_id_type=MESH)

    for step in range(ITERS):
        xs = x.at[step]

        def fill(k, _):
            sampled = mask[k] == 1
            if step == 0:
                value = jnp.where(sampled, measured[k], 0.0)
            else:
                value = combine(step - 1, k, sampled)
            xs[k + 1, c, :, :lanes] = value
            return 0

        def combine(last, k, sampled):
            got = rm[last, planes - 1 - k]
            hi, lo = split(got)
            parts = []
            for q in range(lanes // LANES):
                s = slice(lanes - (q + 1) * LANES, lanes - q * LANES)
                parts.append(jnp.dot(hi[:, s], flip, preferred_element_type=jnp.float32)
                             + jnp.dot(lo[:, s], flip, preferred_element_type=jnp.float32))
            return jnp.where(sampled, measured[k], r1[k] + jnp.concatenate(parts, 1))

        lax.fori_loop(0, planes, fill, 0)

        @pl.when(z == 0)
        def _():
            xs[0, :, :, :lanes] = jnp.zeros((nc, rows, lanes), jnp.float32)

        @pl.when(z == nz - 1)
        def _():
            xs[planes + 1, :, :, :lanes] = jnp.zeros((nc, rows, lanes), jnp.float32)

        if step == 0:
            wh[...], wl[...] = split(weights[...])

        own = xs.at[pl.ds(1, planes), c, :, pl.ds(0, lanes)]
        gathers = [remote(own, own, g_send.at[step, d - 1], g_recv.at[step, d - 1],
                          {"coil": lax.rem(c + d, nc)}) for d in range(1, nc)]
        for copy in gathers:
            copy.start()
        for copy in gathers:
            copy.wait()

        down = remote(xs.at[1, :, :, pl.ds(0, lanes)], xs.at[planes + 1, :, :, pl.ds(0, lanes)],
                      z_send.at[step, 0], z_recv.at[step, 0], {"kz": lax.max(z - 1, 0)})
        up = remote(xs.at[planes, :, :, pl.ds(0, lanes)], xs.at[0, :, :, pl.ds(0, lanes)],
                    z_send.at[step, 1], z_recv.at[step, 1], {"kz": lax.min(z + 1, nz - 1)})

        @pl.when(z > 0)
        def _():
            down.start()

        @pl.when(z < nz - 1)
        def _():
            up.start()

        @pl.when(z > 0)
        def _():
            down.wait_send()
            up.wait_recv()

        @pl.when(z < nz - 1)
        def _():
            up.wait_send()
            down.wait_recv()

        near = pl.multiple_of((1 - h) * (lanes - LANES), LANES)
        side = remote(xs.at[:, :, :, pl.ds(near, LANES)], xs.at[:, :, :, pl.ds(lanes, LANES)],
                      k_send.at[step], k_recv.at[step], {"kx": 1 - h})
        side.start()
        side.wait()

        def divide(k, _):
            value = xs[k].reshape(nc * rows, wide)
            xh[k], xl[k] = split(jnp.where(keep, value, 0.0))
            return 0

        lax.fori_loop(0, planes + 2, divide, 0)

        def send(k):
            return remote(r2.at[step, k], rm.at[step, k], m_send.at[step, k], m_recv.at[step, k], mirror)

        def convolve(k, _):
            hi = xh[pl.ds(k, 3)].reshape(-1, wide)
            lo = xl[pl.ds(k, 3)].reshape(-1, wide)
            results = []
            for v in (1, 0):
                w = slice(v * 9 * rows, (v + 1) * 9 * rows)
                p = (jnp.dot(wh[w], hi, preferred_element_type=jnp.float32)
                     + jnp.dot(wh[w], lo, preferred_element_type=jnp.float32)
                     + jnp.dot(wl[w], hi, preferred_element_type=jnp.float32))
                total = None
                for b in (1, 0, 2):
                    t = p[(3 * b + 1) * rows:(3 * b + 2) * rows]
                    t = t + pltpu.roll(p[3 * b * rows:(3 * b + 1) * rows], row, 1)
                    t = t + pltpu.roll(p[(3 * b + 2) * rows:(3 * b + 3) * rows], wide - row, 1)
                    if b == 0:
                        t = jnp.where(after, pltpu.roll(t, 1, 1), 0.0)
                    if b == 2:
                        t = jnp.where(before, pltpu.roll(t, wide - 1, 1), 0.0)
                    total = t if total is None else total + t
                results.append(total[:, :lanes])
            r2[step, k] = results[0]
            r1[k] = results[1]

            @pl.when(k > 0)
            def _():
                send(k - 1).start()

            return 0

        lax.fori_loop(0, planes, convolve, 0)
        send(planes - 1).start()

        def finish(k, _):
            send(k).wait()
            return 0

        lax.fori_loop(0, planes, finish, 0)

    def last(k, _):
        out[k] = combine(ITERS - 1, k, mask[k] == 1)
        return 0

    lax.fori_loop(0, planes, last, 0)


def on_device(sizes, measured, mask, kernel):
    nz, nc = sizes
    _, coils, depth_x, planes, row = measured.shape
    rows, lanes = 2 * coils, depth_x * row
    wide = lanes + LANES
    weights = build_weights(kernel, nc)
    flat = measured.transpose(3, 0, 1, 2, 4).reshape(planes, rows, lanes)
    sampled = mask.transpose(1, 0, 2).reshape(planes, 1, lanes)
    vmem = pl.BlockSpec(memory_space=pltpu.VMEM)
    dma = pltpu.SemaphoreType.DMA
    result = pl.pallas_call(
        functools.partial(body, sizes, row),
        out_shape=jax.ShapeDtypeStruct((planes, rows, lanes), jnp.float32),
        in_specs=[vmem] * 3,
        out_specs=vmem,
        scratch_shapes=[
            pltpu.VMEM((ITERS, planes + 2, nc, rows, wide), jnp.float32),
            pltpu.VMEM((planes + 2, nc * rows, wide), jnp.bfloat16),
            pltpu.VMEM((planes + 2, nc * rows, wide), jnp.bfloat16),
            pltpu.VMEM(weights.shape, jnp.bfloat16),
            pltpu.VMEM(weights.shape, jnp.bfloat16),
            pltpu.VMEM((planes, rows, lanes), jnp.float32),
            pltpu.VMEM((ITERS, planes, rows, lanes), jnp.float32),
            pltpu.VMEM((ITERS, planes, rows, lanes), jnp.float32),
            dma((ITERS, nc - 1)), dma((ITERS, nc - 1)),
            dma((ITERS, 2)), dma((ITERS, 2)),
            dma((ITERS,)), dma((ITERS,)),
            dma((ITERS, planes)), dma((ITERS, planes)),
        ],
        compiler_params=pltpu.CompilerParams(collective_id=0, has_side_effects=True),
    )(flat, sampled, weights)
    result = result.reshape(planes, 2, coils, depth_x, row)
    return result.transpose(1, 2, 3, 0, 4)


def solution(mesh):
    placed = (
        P(None, ("grp", "coil"), "kx", "kz", None),
        P(("grp", "kx"), "kz", None),
        P(None, None, "coil", None),
    )
    return jax.shard_map(
        functools.partial(on_device, (mesh.shape["kz"], mesh.shape["coil"])),
        mesh=mesh,
        in_specs=placed,
        out_specs=P(None, ("grp", "coil"), "kx", "kz", None),
        check_vma=False,
    )
```

time: 734 us -> 126 us (0.17); the launches traced: 727 us -> 126 us
  waiting for transfers between devices: 397 us -> 0 us
  local copies, waits for them, and re-layouts: 196 us -> 19.5 us
  Pallas kernels: 0 us -> 98.8 us
  other arithmetic: 55.1 us -> 7.62 us
  matrix products: 37.4 us -> 0 us
  starting transfers between devices: 27.1 us -> 0 us
  between operations: 13.7 us -> 0.14 us
    ppermute x14 -> x0, waiting for transfers between devices: 291 us -> none  [the longest x6 282 us: partner(): lax.ppermute(array, axis, [(i, i ^ 1 << apart) for i in range(lax.axis_si...]
    all_gather x4 -> x0, waiting for transfers between devices: 106 us -> none  [the longest x2 106 us: on_device(): lax.all_gather(own_virtual, 'coil', axis=1, tiled=True)]
    pallas_call x0 -> x1, Pallas kernels: none -> 98.8 us  [on_device(): pl.pallas_call(functools.partial(body, sizes, row), out_shape=jax.ShapeDt...]
    squeeze x21 -> x2, local copies, waits for them, and re-layouts: 74.1 us -> 0.92 us  [the longest x1 0.62 us: build_weights(): re, im = (k[:, :, :, 0], k[:, :, :, 1])]
    dot_general x6 -> x0, matrix products: 37.4 us -> none  [convolve(): products = jnp.dot(group, window, precision=lax.Precision.HIGHEST)]
    slice x8 -> x0, local copies, waits for them, and re-layouts: 30.7 us -> none  [the longest x4 17.7 us: padded_2(): last = lax.slice_in_dim(array, length - width, length, axis=dim)]
    ppermute x14 -> x0, starting transfers between devices: 27 us -> none  [the longest x4 12.4 us: padded_2(): after = lax.ppermute(first, axis, down)]
    unnamed x26 -> x3, local copies, waits for them, and re-layouts: 26.3 us -> 0.5 us
  transfers between devices with their start and end apart: 18 -> 0, of which waited for: 13 -> 0; matrix products, arithmetic and copies ran while one was open for 5% -> 0% of each run, Pallas kernels for 0% -> 0%
where the time goes in v1:
time: 126 us
  Pallas kernels  98.8 us (78%)
  local copies, waits for them, and re-layouts  19.5 us (15%)
  other arithmetic  7.62 us (6%)
    pallas_call x1, Pallas kernels, on_device(): pl.pallas_call(functools.partial(body, sizes, row), out_shape=jax.ShapeDt...  98.8 us
    reshape x2, local copies, waits for them, and re-layouts, build_weights(): return w.reshape(36 * coils, 6 * shards * coils)  6.82 us
    reshape x2, local copies, waits for them, and re-layouts, on_device(): result = result.reshape(planes, 2, coils, depth_x, row)  4.17 us
    another operation x3, other arithmetic, block(): return jnp.stack([jnp.stack(row, 0) for row in q], 0)  2.88 us
    reshape x1, local copies, waits for them, and re-layouts, build_weights(): k = kernel.reshape(3, 3, 3, 2, coils, 2, shards, coils)  2.7 us
    transpose x1, other arithmetic, build_weights(): w = w.transpose(0, 4, 3, 1, 6, 5, 7, 2, 8)  2.68 us

profile of v1, /device:TPU:9, one launch (start us, length us, event | category | flops | bytes accessed | tf_op | source)
XLA Modules:
  0.0 126.0 jit_solution(9568309489893225577)
XLA Ops:
  0.0 2.7 %reshape.27 = f32[3,3,3,2,16,2,2,16]{7,6,5,4,3,2,1,0:T(2,128)S(1)} reshape(f32[27,2,16,64]{3,2,1,0:T(8,128)} %param.5) | data formatting | bytes 442368 | tf_op jit(solution)/shard_map/reshape | solution.py:17
  2.7 0.6 slice_bitcast_fusion
  3.3 0.3 slice_bitcast_fusion.3
  3.6 0.5 copy.43
  4.1 0.1 slice_bitcast_fusion.4
  4.2 0.7 reverse_bitcast_fusion.1
  4.9 1.0 maximum_bitcast_fusion.5
  5.9 0.9 maximum_bitcast_fusion.2
  6.8 0.2 fusion
  7.0 1.2 maximum_bitcast_fusion.3
  8.3 0.9 maximum_bitcast_fusion.1
  9.2 2.7 %maximum_bitcast_fusion = f32[2,3,3,2,16,3,2,2,16]{8,6,4,5,1,2,7,3,0:T(2,128)S(1)} fusion(f32[1,2,2,3,3,3,16,2,16]{8,7,6,5,4,3,2,1,0:T(2,128)S(1)} %maximum_bitcast_fusion.2, f32[1,2,2,3,3,3,16,2,16]{8,7,6,5,4,3,2,1,0:T(2,128)S(1)} %maximum_bitcast_fusion.1), kind=kLoop, calls=%fused_computation | loop fusion | flops 110592 | bytes 884736 | tf_op jit(solution)/shard_map/transpose | solution.py:26
  11.9 2.9 %copy.36 = f32[2,3,3,2,16,3,2,2,16]{8,7,6,5,4,3,2,1,0:T(2,128)S(1)} copy(f32[2,3,3,2,16,3,2,2,16]{8,6,4,5,1,2,7,3,0:T(2,128)S(1)} %maximum_bitcast_fusion) | data formatting | bytes 884736 | tf_op jit(solution)/shard_map/reshape | solution.py:27
  14.8 3.9 %reshape.30.weights = f32[576,192]{1,0:T(8,128)} reshape(f32[2,3,3,2,16,3,2,2,16]{8,7,6,5,4,3,2,1,0:T(2,128)S(1)} %copy.36) | data formatting | bytes 884736 | tf_op jit(solution)/shard_map/reshape | solution.py:27
  18.7 2.0 %copy.26 = f32[8,2,16,16,32]{4,3,2,1,0:T(8,128)S(1)} copy(f32[8,2,16,16,32]{4,0,3,2,1:T(8,128)} %bitcast.47) | data formatting | bytes 1048576 | tf_op jit(solution)/shard_map/transpose | solution.py:199
  20.7 0.0 copy-start
  20.7 1.6 %reshape.25.measured = f32[8,32,512]{2,1,0:T(8,128)} reshape(f32[8,2,16,16,32]{4,3,2,1,0:T(8,128)S(1)} %copy.26) | data formatting | bytes 1048576 | tf_op jit(solution)/shard_map/reshape | solution.py:199
  22.3 0.0 copy-done
  22.3 0.7 reshape.26.mask
  23.0 98.8 %shard_map.37 = f32[8,32,512]{2,1,0:T(8,128)} custom-call(f32[8,32,512]{2,1,0:T(8,128)} %reshape.25.measured, s32[8,1,512]{2,1,0:T(1,128)} %reshape.26.mask, f32[576,192]{1,0:T(8,128)} %reshape.30.weights), custom_call_target="tpu_custom_call" | custom-call | tf_op jit(solution)/shard_map/pallas_call | solution.py:203
  121.9 1.6 %reshape.29 = f32[8,2,16,16,32]{4,3,2,1,0:T(8,128)S(1)} reshape(f32[8,32,512]{2,1,0:T(8,128)} %shard_map.37) | data formatting | bytes 1048576 | tf_op jit(solution)/shard_map/reshape | solution.py:224
  123.5 2.5 %copy.42 = f32[8,2,16,16,32]{4,0,3,2,1:T(8,128)} copy(f32[8,2,16,16,32]{4,3,2,1,0:T(8,128)S(1)} %reshape.29) | data formatting | bytes 1048576 | tf_op jit(solution)/shard_map/reshape | solution.py:224
  (1 shorter events, 0.0 us)
Async XLA Ops:
  20.7 1.6 %copy-start = (s32[16,8,32]{2,1,0:T(8,128)S(1)}, s32[16,8,32]{2,1,0:T(8,128)}, u32[]{:S(2)}) copy-start(s32[16,8,32]{2,1,0:T(8,128)} %param.4) | copy-start | bytes 49156

commit v2 on v1

v2 whole, which is shorter than its diff:
```python
import functools

import jax
import jax.numpy as jnp
from jax import lax
from jax.experimental import pallas as pl
from jax.experimental.pallas import tpu as pltpu
from jax.sharding import PartitionSpec as P

ITERS = 2
LANES = 128
MESH = pl.DeviceIdType.MESH


def order(n, count, turn):
    odd = (n + turn) % 2
    return (1 - odd) * (count // 2 - 1 - n // 2) + odd * (count // 2 + n // 2)


def place_weights(kernel, shards, wf, target, low):
    taps, _, coils, inputs = kernel.shape
    width = 2 * inputs
    half = inputs // 2
    shape = (inputs, 2 * width)
    d = lax.broadcasted_iota(jnp.int32, shape, 0)
    q = lax.broadcasted_iota(jnp.int32, shape, 1)
    v, po = q // width, (q // inputs) % 2
    at = q % inputs
    pi, source = (at // coils) % 2, v * half + (at // (2 * coils)) * coils + at % coils
    hit = d == source
    real = jnp.where(hit & (po == pi), jnp.where((v == 1) & (po == 1), -1.0, 1.0), 0.0).astype(jnp.bfloat16)
    imag = jnp.where(hit & (po != pi), jnp.where((v == 0) & (po == 0), -1.0, 1.0), 0.0).astype(jnp.bfloat16)
    picked = (jnp.dot(split(kernel[:, 0].reshape(taps * coils, inputs))[low], real, preferred_element_type=jnp.float32)
              + jnp.dot(split(kernel[:, 1].reshape(taps * coils, inputs))[low], imag, preferred_element_type=jnp.float32))
    for v in range(2):
        for b in range(3):
            for a in range(3):
                for po in range(2):
                    parts = []
                    for e in range(3):
                        t = 9 * a + 3 * b + e
                        t = taps - 1 - t if v else t
                        parts.append(picked[t * coils:(t + 1) * coils, (2 * v + po) * inputs:(2 * v + po + 1) * inputs])
                    first = (((v * 3 + b) * 3 + a) * 2 + po) * coils
                    wf[first:first + coils, :] = jnp.concatenate(parts, 1)
    target[...] = wf[...].astype(jnp.bfloat16)


def split(x):
    hi = x.astype(jnp.bfloat16)
    return hi, (x - hi.astype(jnp.float32)).astype(jnp.bfloat16)


def body(sizes, row, measured, mask, kernel, out, x, xh, xl, wf, wh, wl, r1, r2, rm,
         g_send, g_recv, z_send, z_recv, k_send, k_recv, m_send, m_recv):
    nz, nc = sizes
    planes, rows, lanes = measured.shape
    wide = lanes + LANES
    z, c, h = lax.axis_index("kz"), lax.axis_index("coil"), lax.axis_index("kx")
    mirror = {"kz": nz - 1 - z, "kx": 1 - h}

    barrier = pltpu.get_barrier_semaphore()
    for d in range(1, nc):
        pl.semaphore_signal(barrier, inc=1, device_id={"coil": lax.rem(c + d, nc)}, device_id_type=MESH)
    pl.semaphore_signal(barrier, inc=1, device_id={"kx": 1 - h}, device_id_type=MESH)
    pl.semaphore_signal(barrier, inc=1, device_id=mirror, device_id_type=MESH)

    for d in (1, nz - 1):
        pl.semaphore_signal(barrier, inc=1, device_id={"kz": lax.rem(z + d, nz)}, device_id_type=MESH)
    pl.semaphore_wait(barrier, nc + 3)

    lane = lax.broadcasted_iota(jnp.int32, (1, wide), 1)
    edge = lane - lanes - h * (LANES - row)
    keep = (lane < lanes) | ((edge >= 0) & (edge < row))
    column = lax.rem(lane, row)
    after, before = column > 0, column < row - 1
    flip = (lax.broadcasted_iota(jnp.int32, (LANES, LANES), 0)
            + lax.broadcasted_iota(jnp.int32, (LANES, LANES), 1) == LANES - 1)
    flip = flip.astype(jnp.float32).astype(jnp.bfloat16)

    def remote(src, dst, send, recv, device):
        return pltpu.make_async_remote_copy(
            src_ref=src, dst_ref=dst, send_sem=send, recv_sem=recv, device_id=device, device_id_type=MESH)

    slots = planes + 2

    def combine(step, k):
        sampled = mask[k] == 1
        hi, lo = split(rm[step, k])
        parts = []
        for q in range(lanes // LANES):
            s = slice(lanes - (q + 1) * LANES, lanes - q * LANES)
            parts.append(jnp.dot(hi[:, s], flip, preferred_element_type=jnp.float32)
                         + jnp.dot(lo[:, s], flip, preferred_element_type=jnp.float32))
        return jnp.where(sampled, measured[k], r1[k] + jnp.concatenate(parts, 1))

    def gather(step, slot, d):
        own = x.at[step, slot, c, :, pl.ds(0, lanes)]
        return remote(own, own, g_send.at[step, d - 1, slot], g_recv.at[step, d - 1, slot],
                      {"coil": lax.rem(c + d, nc)})

    def outer(step):
        down = remote(x.at[step, 1, c, :, pl.ds(0, lanes)], x.at[step, planes + 1, c, :, pl.ds(0, lanes)],
                      z_send.at[step, 0], z_recv.at[step, 0], {"kz": lax.max(z - 1, 0)})
        up = remote(x.at[step, planes, c, :, pl.ds(0, lanes)], x.at[step, 0, c, :, pl.ds(0, lanes)],
                    z_send.at[step, 1], z_recv.at[step, 1], {"kz": lax.min(z + 1, nz - 1)})
        return down, up

    def side(step, slot):
        near = pl.multiple_of((1 - h) * (lanes - LANES), LANES)
        return remote(x.at[step, slot, :, :, pl.ds(near, LANES)], x.at[step, slot, :, :, pl.ds(lanes, LANES)],
                      k_send.at[step, slot], k_recv.at[step, slot], {"kx": 1 - h})

    def send(step, k):
        return remote(r2.at[step, k], rm.at[step, planes - 1 - k], m_send.at[step, k],
                      m_recv.at[step, planes - 1 - k], mirror)

    def receive(step, k):
        remote(r2.at[step, planes - 1 - k], rm.at[step, k], m_send.at[step, planes - 1 - k],
               m_recv.at[step, k], mirror).wait_recv()

    def start_outer(step):
        down, up = outer(step)

        @pl.when(z > 0)
        def _():
            down.start()

        @pl.when(z < nz - 1)
        def _():
            up.start()

    def wait_outer(step):
        down, up = outer(step)

        @pl.when(z > 0)
        def _():
            down.wait_send()
            up.wait_recv()

        @pl.when(z < nz - 1)
        def _():
            up.wait_send()
            down.wait_recv()

    def start_gather(step, n):
        for d in range(1, nc):
            gather(step, order(n, slots, step), d).start()

    def wait_gather(step, n):
        slot = order(n, slots, step)
        for d in range(1, nc):
            gather(step, slot, d).wait_recv()
        side(step, slot).start()

    def divide(step, n):
        slot = order(n, slots, step)
        side(step, slot).wait_recv()
        value = x[step, slot].reshape(nc * rows, wide)
        xh[slot], xl[slot] = split(jnp.where(keep, value, 0.0))

    def convolve(step, n):
        k = order(n, slots, step) - 1
        hi = xh[pl.ds(k, 3)].reshape(-1, wide)
        lo = xl[pl.ds(k, 3)].reshape(-1, wide)
        results = []
        for v in (1, 0):
            w = slice(v * 9 * rows, (v + 1) * 9 * rows)
            p = (jnp.dot(wh[w], hi, preferred_element_type=jnp.float32)
                 + jnp.dot(wh[w], lo, preferred_element_type=jnp.float32)
                 + jnp.dot(wl[w], hi, preferred_element_type=jnp.float32))
            total = None
            for b in (1, 0, 2):
                t = p[(3 * b + 1) * rows:(3 * b + 2) * rows]
                t = t + pltpu.roll(p[3 * b * rows:(3 * b + 1) * rows], row, 1)
                t = t + pltpu.roll(p[(3 * b + 2) * rows:(3 * b + 3) * rows], wide - row, 1)
                if b == 0:
                    t = jnp.where(after, pltpu.roll(t, 1, 1), 0.0)
                if b == 2:
                    t = jnp.where(before, pltpu.roll(t, wide - 1, 1), 0.0)
                total = t if total is None else total + t
            results.append(total[:, :lanes])
            if v:
                r2[step, k] = results[0]
        r1[k] = results[1]
        send(step, k).start()

    for step in range(ITERS):
        @pl.when(z == 0)
        def _():
            x[step, 0, c, :, :lanes] = jnp.zeros((rows, lanes), jnp.float32)

        @pl.when(z == nz - 1)
        def _():
            x[step, planes + 1, c, :, :lanes] = jnp.zeros((rows, lanes), jnp.float32)

    def first(k, _):
        x[0, k + 1, c, :, :lanes] = jnp.where(mask[k] == 1, measured[k], 0.0)
        return 0

    lax.fori_loop(0, planes, first, 0)
    start_outer(0)

    def first_gather(n, _):
        start_gather(0, n)
        return 0

    lax.fori_loop(0, planes, first_gather, 0)
    place_weights(kernel, nc, wf, wh, 0)
    wait_outer(0)
    lax.fori_loop(planes, slots, first_gather, 0)
    place_weights(kernel, nc, wf, wl, 1)

    for step in range(ITERS):
        lag = 1 if step else 0

        def stage(n, _):
            if step:
                @pl.when(n < planes)
                def _():
                    k = order(n, slots, step) - 1
                    receive(step - 1, k)
                    x[step, k + 1, c, :, :lanes] = combine(step - 1, k)

                @pl.when(n == planes)
                def _():
                    start_outer(step)
                    wait_outer(step)

            @pl.when((n >= 1 + lag) & (n < slots + 1 + lag))
            def _():
                divide(step, n - 1 - lag)

            if step:
                @pl.when(n < slots)
                def _():
                    start_gather(step, n)

            @pl.when((n >= lag) & (n < slots + lag))
            def _():
                wait_gather(step, n - lag)

            @pl.when(n >= 3 + lag)
            def _():
                convolve(step, n - 3 - lag)

            return 0

        lax.fori_loop(0, planes + 3 + lag, stage, 0)

    def last(n, _):
        k = order(n, slots, ITERS) - 1
        receive(ITERS - 1, k)
        out[k] = combine(ITERS - 1, k)
        return 0

    lax.fori_loop(0, planes, last, 0)

    for step in range(ITERS):
        def sent(slot, _):
            for d in range(1, nc):
                gather(step, slot, d).wait_send()
            side(step, slot).wait_send()
            return 0

        lax.fori_loop(0, slots, sent, 0)

        def mirrored(k, _):
            send(step, k).wait_send()
            return 0

        lax.fori_loop(0, planes, mirrored, 0)


def on_device(sizes, measured, mask, kernel):
    nz, nc = sizes
    _, coils, depth_x, planes, row = measured.shape
    rows, lanes = 2 * coils, depth_x * row
    wide = lanes + LANES
    flat = measured.transpose(3, 0, 1, 2, 4).reshape(planes, rows, lanes)
    sampled = mask.transpose(1, 0, 2).reshape(planes, 1, lanes)
    weights = (18 * rows, 3 * nc * rows)
    vmem = pl.BlockSpec(memory_space=pltpu.VMEM)
    dma = pltpu.SemaphoreType.DMA
    result = pl.pallas_call(
        functools.partial(body, sizes, row),
        out_shape=jax.ShapeDtypeStruct((planes, rows, lanes), jnp.float32),
        in_specs=[vmem] * 3,
        out_specs=vmem,
        scratch_shapes=[
            pltpu.VMEM((ITERS, planes + 2, nc, rows, wide), jnp.float32),
            pltpu.VMEM((planes + 2, nc * rows, wide), jnp.bfloat16),
            pltpu.VMEM((planes + 2, nc * rows, wide), jnp.bfloat16),
            pltpu.VMEM(weights, jnp.float32),
            pltpu.VMEM(weights, jnp.bfloat16),
            pltpu.VMEM(weights, jnp.bfloat16),
            pltpu.VMEM((planes, rows, lanes), jnp.float32),
            pltpu.VMEM((ITERS, planes, rows, lanes), jnp.float32),
            pltpu.VMEM((ITERS, planes, rows, lanes), jnp.float32),
            dma((ITERS, nc - 1, planes + 2)), dma((ITERS, nc - 1, planes + 2)),
            dma((ITERS, 2)), dma((ITERS, 2)),
            dma((ITERS, planes + 2)), dma((ITERS, planes + 2)),
            dma((ITERS, planes)), dma((ITERS, planes)),
        ],
        compiler_params=pltpu.CompilerParams(collective_id=0, has_side_effects=True),
    )(flat, sampled, kernel)
    result = result.reshape(planes, 2, coils, depth_x, row)
    return result.transpose(1, 2, 3, 0, 4)


def solution(mesh):
    placed = (
        P(None, ("grp", "coil"), "kx", "kz", None),
        P(("grp", "kx"), "kz", None),
        P(None, None, "coil", None),
    )
    return jax.shard_map(
        functools.partial(on_device, (mesh.shape["kz"], mesh.shape["coil"])),
        mesh=mesh,
        in_specs=placed,
        out_specs=P(None, ("grp", "coil"), "kx", "kz", None),
        check_vma=False,
    )
```

time: 126 us -> 74.7 us (0.59)
  Pallas kernels: 98.8 us -> 65.2 us
  local copies, waits for them, and re-layouts: 19.5 us -> 9.3 us
  other arithmetic: 7.62 us -> 0 us
    pallas_call x1, Pallas kernels: 98.8 us -> 65.2 us  [on_device(): pl.pallas_call(functools.partial(body, sizes, row), out_shape=jax.ShapeDt...]
    reshape x3 -> x0, local copies, waits for them, and re-layouts: 9.52 us -> none  [the longest x2 6.82 us: build_weights(): return w.reshape(36 * coils, 6 * shards * coils)]
    another operation x5 -> x0, other arithmetic: 4.71 us -> none  [the longest x3 2.88 us: block(): return jnp.stack([jnp.stack(row, 0) for row in q], 0)]
    transpose x1 -> x0, other arithmetic: 2.68 us -> none  [build_weights(): w = w.transpose(0, 4, 3, 1, 6, 5, 7, 2, 8)]
where the time goes in v2:
time: 74.7 us; the launch traced here: 74.5 us
  Pallas kernels  65.2 us (87%)
  local copies, waits for them, and re-layouts  9.3 us (12%)
    pallas_call x1, Pallas kernels, on_device(): pl.pallas_call(functools.partial(body, sizes, row), out_shape=jax.ShapeDt...  65.2 us
    reshape x2, local copies, waits for them, and re-layouts, on_device(): result = result.reshape(planes, 2, coils, depth_x, row)  4.17 us
    transpose x1, local copies, waits for them, and re-layouts, on_device(): flat = measured.transpose(3, 0, 1, 2, 4).reshape(planes, rows, lanes)  2 us
    reshape x1, local copies, waits for them, and re-layouts, on_device(): flat = measured.transpose(3, 0, 1, 2, 4).reshape(planes, rows, lanes)  1.58 us

profile of v2, /device:TPU:9, one launch (start us, length us, event | category | flops | bytes accessed | tf_op | source)
XLA Modules:
  0.0 74.5 jit_solution(3099612037747989966)
XLA Ops:
  0.0 0.9 %copy.5 = s32[8,16,32]{2,1,0:T(8,128)S(1)} copy(s32[8,16,32]{2,0,1:T(8,128)} %bitcast.8) | data formatting | bytes 32768 | tf_op jit(solution)/shard_map/transpose | solution.py:281
  0.9 0.7 reshape.10.mask
  1.5 2.0 %copy.4 = f32[8,2,16,16,32]{4,3,2,1,0:T(8,128)S(1)} copy(f32[8,2,16,16,32]{4,0,3,2,1:T(8,128)} %bitcast.7) | data formatting | bytes 1048576 | tf_op jit(solution)/shard_map/transpose | solution.py:280
  3.5 1.6 %reshape.9.measured = f32[8,32,512]{2,1,0:T(8,128)} reshape(f32[8,2,16,16,32]{4,3,2,1,0:T(8,128)S(1)} %copy.4) | data formatting | bytes 1048576 | tf_op jit(solution)/shard_map/reshape | solution.py:280
  5.1 65.2 %shard_map.37 = f32[8,32,512]{2,1,0:T(8,128)} custom-call(f32[8,32,512]{2,1,0:T(8,128)} %reshape.9.measured, s32[8,1,512]{2,1,0:T(1,128)} %reshape.10.mask, f32[27,2,16,64]{3,2,1,0:T(8,128)} %kernel.1), custom_call_target="tpu_custom_call" | custom-call | tf_op jit(solution)/shard_map/pallas_call | solution.py:285
  70.3 1.6 %reshape.11 = f32[8,2,16,16,32]{4,3,2,1,0:T(8,128)S(1)} reshape(f32[8,32,512]{2,1,0:T(8,128)} %shard_map.37) | data formatting | bytes 1048576 | tf_op jit(solution)/shard_map/reshape | solution.py:307
  72.0 2.5 %copy.8 = f32[8,2,16,16,32]{4,0,3,2,1:T(8,128)} copy(f32[8,2,16,16,32]{4,3,2,1,0:T(8,128)S(1)} %reshape.11) | data formatting | bytes 1048576 | tf_op jit(solution)/shard_map/reshape | solution.py:307

commit v3 on v2

--- a/solution.py
+++ b/solution.py
@@ -211,42 +211,66 @@
     lax.fori_loop(planes, slots, first_gather, 0)
     place_weights(kernel, nc, wf, wl, 1)
 
-    for step in range(ITERS):
-        lag = 1 if step else 0
-
-        def stage(n, _):
-            if step:
-                @pl.when(n < planes)
-                def _():
-                    k = order(n, slots, step) - 1
-                    receive(step - 1, k)
-                    x[step, k + 1, c, :, :lanes] = combine(step - 1, k)
-
-                @pl.when(n == planes)
-                def _():
-                    start_outer(step)
-                    wait_outer(step)
-
-            @pl.when((n >= 1 + lag) & (n < slots + 1 + lag))
-            def _():
-                divide(step, n - 1 - lag)
-
-            if step:
-                @pl.when(n < slots)
-                def _():
-                    start_gather(step, n)
-
-            @pl.when((n >= lag) & (n < slots + lag))
-            def _():
-                wait_gather(step, n - lag)
-
-            @pl.when(n >= 3 + lag)
-            def _():
-                convolve(step, n - 3 - lag)
+    def stage(n, _):
+        @pl.when((n >= 1) & (n < slots + 1))
+        def _():
+            divide(0, n - 1)
+
+        @pl.when(n < slots)
+        def _():
+            wait_gather(0, n)
+
+        @pl.when(n >= 3)
+        def _():
+            convolve(0, n - 3)
+
+        return 0
+
+    lax.fori_loop(0, planes + 3, stage, 0)
+
+    for step in range(1, ITERS):
+        def again(n, _):
+            @pl.when(n < planes)
+            def _():
+                k = order(n, slots, step) - 1
+                receive(step - 1, k)
+                x[step, k + 1, c, :, :lanes] = combine(step - 1, k)
+
+            @pl.when(n >= 2)
+            def _():
+                divide(step, n - 2)
+
+            @pl.when(n == planes - 1)
+            def _():
+                start_outer(step)
+
+            @pl.when(n < planes)
+            def _():
+                start_gather(step, n)
+
+            @pl.when((n >= 1) & (n < planes + 1))
+            def _():
+                wait_gather(step, n - 1)
+
+            @pl.when(n >= 4)
+            def _():
+                convolve(step, n - 4)
 
             return 0
 
-        lax.fori_loop(0, planes + 3 + lag, stage, 0)
+        lax.fori_loop(0, planes + 2, again, 0)
+        wait_outer(step)
+        for n in (planes, planes + 1):
+            start_gather(step, n)
+        for n in (planes, planes + 1):
+            wait_gather(step, n)
+
+        def rest(n, _):
+            divide(step, n + 2)
+            convolve(step, n)
+            return 0
+
+        lax.fori_loop(planes - 2, planes, rest, 0)
 
     def last(n, _):
         k = order(n, slots, ITERS) - 1

time: 74.7 us -> 75.4 us (level)
  no operation moved by 1% of the time
where the time goes in v3:
time: 75.4 us; the launch traced here: 74.6 us
  Pallas kernels  65.2 us (86%)
  local copies, waits for them, and re-layouts  9.3 us (12%)
    pallas_call x1, Pallas kernels, on_device(): pl.pallas_call(functools.partial(body, sizes, row), out_shape=jax.ShapeDt...  65.2 us
    reshape x2, local copies, waits for them, and re-layouts, on_device(): result = result.reshape(planes, 2, coils, depth_x, row)  4.17 us
    transpose x1, local copies, waits for them, and re-layouts, on_device(): flat = measured.transpose(3, 0, 1, 2, 4).reshape(planes, rows, lanes)  2 us
    reshape x1, local copies, waits for them, and re-layouts, on_device(): flat = measured.transpose(3, 0, 1, 2, 4).reshape(planes, rows, lanes)  1.58 us

profile of v3, /device:TPU:9, one launch (start us, length us, event | category | flops | bytes accessed | tf_op | source)
XLA Modules:
  0.0 74.6 jit_solution(15122676504450378174)
XLA Ops:
  0.0 0.9 %copy.5 = s32[8,16,32]{2,1,0:T(8,128)S(1)} copy(s32[8,16,32]{2,0,1:T(8,128)} %bitcast.8) | data formatting | bytes 32768 | tf_op jit(solution)/shard_map/transpose | solution.py:305
  0.9 0.7 reshape.10.mask
  1.5 2.0 %copy.4 = f32[8,2,16,16,32]{4,3,2,1,0:T(8,128)S(1)} copy(f32[8,2,16,16,32]{4,0,3,2,1:T(8,128)} %bitcast.7) | data formatting | bytes 1048576 | tf_op jit(solution)/shard_map/transpose | solution.py:304
  3.5 1.6 %reshape.9.measured = f32[8,32,512]{2,1,0:T(8,128)} reshape(f32[8,2,16,16,32]{4,3,2,1,0:T(8,128)S(1)} %copy.4) | data formatting | bytes 1048576 | tf_op jit(solution)/shard_map/reshape | solution.py:304
  5.1 65.2 %shard_map.37 = f32[8,32,512]{2,1,0:T(8,128)} custom-call(f32[8,32,512]{2,1,0:T(8,128)} %reshape.9.measured, s32[8,1,512]{2,1,0:T(1,128)} %reshape.10.mask, f32[27,2,16,64]{3,2,1,0:T(8,128)} %kernel.1), custom_call_target="tpu_custom_call" | custom-call | tf_op jit(solution)/shard_map/pallas_call | solution.py:309
  70.4 1.6 %reshape.11 = f32[8,2,16,16,32]{4,3,2,1,0:T(8,128)S(1)} reshape(f32[8,32,512]{2,1,0:T(8,128)} %shard_map.37) | data formatting | bytes 1048576 | tf_op jit(solution)/shard_map/reshape | solution.py:331
  72.0 2.5 %copy.8 = f32[8,2,16,16,32]{4,0,3,2,1:T(8,128)} copy(f32[8,2,16,16,32]{4,3,2,1,0:T(8,128)S(1)} %reshape.11) | data formatting | bytes 1048576 | tf_op jit(solution)/shard_map/reshape | solution.py:331

commit v4 on v3

--- a/solution.py
+++ b/solution.py
@@ -209,24 +209,26 @@
     place_weights(kernel, nc, wf, wh, 0)
     wait_outer(0)
     lax.fori_loop(planes, slots, first_gather, 0)
+    for n in (0, 1):
+        wait_gather(0, n)
     place_weights(kernel, nc, wf, wl, 1)
 
     def stage(n, _):
-        @pl.when((n >= 1) & (n < slots + 1))
-        def _():
-            divide(0, n - 1)
+        @pl.when(n < slots + 2)
+        def _():
+            divide(0, n - 2)
+
+        @pl.when(n >= 4)
+        def _():
+            convolve(0, n - 4)
 
         @pl.when(n < slots)
         def _():
             wait_gather(0, n)
 
-        @pl.when(n >= 3)
-        def _():
-            convolve(0, n - 3)
-
         return 0
 
-    lax.fori_loop(0, planes + 3, stage, 0)
+    lax.fori_loop(2, planes + 4, stage, 0)
 
     for step in range(1, ITERS):
         def again(n, _):

time: 75.4 us -> 74.9 us (level)
  no operation moved by 1% of the time
where the time goes in v4:
time: 74.9 us; the launch traced here: 74.7 us
  Pallas kernels  65.4 us (87%)
  local copies, waits for them, and re-layouts  9.3 us (12%)
    pallas_call x1, Pallas kernels, on_device(): pl.pallas_call(functools.partial(body, sizes, row), out_shape=jax.ShapeDt...  65.4 us
    reshape x2, local copies, waits for them, and re-layouts, on_device(): result = result.reshape(planes, 2, coils, depth_x, row)  4.17 us
    transpose x1, local copies, waits for them, and re-layouts, on_device(): flat = measured.transpose(3, 0, 1, 2, 4).reshape(planes, rows, lanes)  2 us
    reshape x1, local copies, waits for them, and re-layouts, on_device(): flat = measured.transpose(3, 0, 1, 2, 4).reshape(planes, rows, lanes)  1.58 us

profile of v4, /device:TPU:9, one launch (start us, length us, event | category | flops | bytes accessed | tf_op | source)
XLA Modules:
  0.0 74.7 jit_solution(10251631024042747405)
XLA Ops:
  0.0 0.9 %copy.5 = s32[8,16,32]{2,1,0:T(8,128)S(1)} copy(s32[8,16,32]{2,0,1:T(8,128)} %bitcast.8) | data formatting | bytes 32768 | tf_op jit(solution)/shard_map/transpose | solution.py:307
  0.9 0.7 reshape.10.mask
  1.5 2.0 %copy.4 = f32[8,2,16,16,32]{4,3,2,1,0:T(8,128)S(1)} copy(f32[8,2,16,16,32]{4,0,3,2,1:T(8,128)} %bitcast.7) | data formatting | bytes 1048576 | tf_op jit(solution)/shard_map/transpose | solution.py:306
  3.5 1.6 %reshape.9.measured = f32[8,32,512]{2,1,0:T(8,128)} reshape(f32[8,2,16,16,32]{4,3,2,1,0:T(8,128)S(1)} %copy.4) | data formatting | bytes 1048576 | tf_op jit(solution)/shard_map/reshape | solution.py:306
  5.1 65.4 %shard_map.37 = f32[8,32,512]{2,1,0:T(8,128)} custom-call(f32[8,32,512]{2,1,0:T(8,128)} %reshape.9.measured, s32[8,1,512]{2,1,0:T(1,128)} %reshape.10.mask, f32[27,2,16,64]{3,2,1,0:T(8,128)} %kernel.1), custom_call_target="tpu_custom_call" | custom-call | tf_op jit(solution)/shard_map/pallas_call | solution.py:311
  70.5 1.6 %reshape.11 = f32[8,2,16,16,32]{4,3,2,1,0:T(8,128)S(1)} reshape(f32[8,32,512]{2,1,0:T(8,128)} %shard_map.37) | data formatting | bytes 1048576 | tf_op jit(solution)/shard_map/reshape | solution.py:333
  72.2 2.5 %copy.8 = f32[8,2,16,16,32]{4,0,3,2,1:T(8,128)} copy(f32[8,2,16,16,32]{4,3,2,1,0:T(8,128)S(1)} %reshape.11) | data formatting | bytes 1048576 | tf_op jit(solution)/shard_map/reshape | solution.py:333

commit v5 on v4

--- a/solution.py
+++ b/solution.py
@@ -238,9 +238,9 @@
                 receive(step - 1, k)
                 x[step, k + 1, c, :, :lanes] = combine(step - 1, k)
 
-            @pl.when(n >= 2)
-            def _():
-                divide(step, n - 2)
+            @pl.when((n >= 3) & (n < planes + 3))
+            def _():
+                divide(step, n - 3)
 
             @pl.when(n == planes - 1)
             def _():
@@ -250,20 +250,23 @@
             def _():
                 start_gather(step, n)
 
-            @pl.when((n >= 1) & (n < planes + 1))
-            def _():
-                wait_gather(step, n - 1)
-
-            @pl.when(n >= 4)
-            def _():
-                convolve(step, n - 4)
+            @pl.when(n == planes + 1)
+            def _():
+                wait_outer(step)
+                start_gather(step, planes)
+                start_gather(step, planes + 1)
+
+            @pl.when(n >= 5)
+            def _():
+                convolve(step, n - 5)
+
+            @pl.when((n >= 2) & (n < planes + 2))
+            def _():
+                wait_gather(step, n - 2)
 
             return 0
 
-        lax.fori_loop(0, planes + 2, again, 0)
-        wait_outer(step)
-        for n in (planes, planes + 1):
-            start_gather(step, n)
+        lax.fori_loop(0, planes + 3, again, 0)
         for n in (planes, planes + 1):
             wait_gather(step, n)
 

time: 74.9 us -> 73.2 us (0.977)
  Pallas kernels: 65.4 us -> 63.5 us
    pallas_call x1, Pallas kernels: 65.4 us -> 63.5 us  [on_device(): pl.pallas_call(functools.partial(body, sizes, row), out_shape=jax.ShapeDt...]
where the time goes in v5:
time: 73.2 us; the launch traced here: 72.8 us
  Pallas kernels  63.5 us (87%)
  local copies, waits for them, and re-layouts  9.3 us (13%)
    pallas_call x1, Pallas kernels, on_device(): pl.pallas_call(functools.partial(body, sizes, row), out_shape=jax.ShapeDt...  63.5 us
    reshape x2, local copies, waits for them, and re-layouts, on_device(): result = result.reshape(planes, 2, coils, depth_x, row)  4.17 us
    transpose x1, local copies, waits for them, and re-layouts, on_device(): flat = measured.transpose(3, 0, 1, 2, 4).reshape(planes, rows, lanes)  2 us
    reshape x1, local copies, waits for them, and re-layouts, on_device(): flat = measured.transpose(3, 0, 1, 2, 4).reshape(planes, rows, lanes)  1.58 us

profile of v5, /device:TPU:9, one launch (start us, length us, event | category | flops | bytes accessed | tf_op | source)
XLA Modules:
  0.0 72.8 jit_solution(5729948511999352936)
XLA Ops:
  0.0 0.9 %copy.5 = s32[8,16,32]{2,1,0:T(8,128)S(1)} copy(s32[8,16,32]{2,0,1:T(8,128)} %bitcast.8) | data formatting | bytes 32768 | tf_op jit(solution)/shard_map/transpose | solution.py:310
  0.9 0.7 reshape.10.mask
  1.5 2.0 %copy.4 = f32[8,2,16,16,32]{4,3,2,1,0:T(8,128)S(1)} copy(f32[8,2,16,16,32]{4,0,3,2,1:T(8,128)} %bitcast.7) | data formatting | bytes 1048576 | tf_op jit(solution)/shard_map/transpose | solution.py:309
  3.5 1.6 %reshape.9.measured = f32[8,32,512]{2,1,0:T(8,128)} reshape(f32[8,2,16,16,32]{4,3,2,1,0:T(8,128)S(1)} %copy.4) | data formatting | bytes 1048576 | tf_op jit(solution)/shard_map/reshape | solution.py:309
  5.1 63.5 %shard_map.37 = f32[8,32,512]{2,1,0:T(8,128)} custom-call(f32[8,32,512]{2,1,0:T(8,128)} %reshape.9.measured, s32[8,1,512]{2,1,0:T(1,128)} %reshape.10.mask, f32[27,2,16,64]{3,2,1,0:T(8,128)} %kernel.1), custom_call_target="tpu_custom_call" | custom-call | tf_op jit(solution)/shard_map/pallas_call | solution.py:314
  68.6 1.6 %reshape.11 = f32[8,2,16,16,32]{4,3,2,1,0:T(8,128)S(1)} reshape(f32[8,32,512]{2,1,0:T(8,128)} %shard_map.37) | data formatting | bytes 1048576 | tf_op jit(solution)/shard_map/reshape | solution.py:336
  70.2 2.5 %copy.8 = f32[8,2,16,16,32]{4,0,3,2,1:T(8,128)} copy(f32[8,2,16,16,32]{4,3,2,1,0:T(8,128)S(1)} %reshape.11) | data formatting | bytes 1048576 | tf_op jit(solution)/shard_map/reshape | solution.py:336
